TPU v7x, 128 devices: a whole 4x4x4 slice. The times are simulated.
128 devices in a mesh: pb: 16 (over x, z_lo, core), kv: 8 (over z_hi, y).
Axes of the slice: x: 4, y: 4, z: 4 (z_hi: 2, z_lo: 2; z = z_hi * 2 + z_lo), core: 2. Of those that a mesh axis runs over, the one named last changes fastest.
Arguments:
- queries: float32 [16384, 256], P(('pb', 'kv')), may hold values from -200 to 200
- keys: float32 [16384, 256], P(('pb', 'kv')), may hold values from -8 to 8
- values: float32 [16384, 256], P(('pb', 'kv')), may hold values from -192 to 192
- query_tangent: float32 [16384, 256], P(('pb', 'kv')), may hold values from -6 to 6
- key_tangent: float32 [16384, 256], P(('pb', 'kv')), may hold values from -6 to 6
- value_tangent: float32 [16384, 256], P(('pb', 'kv')), may hold values from -192 to 192
Outputs:
- attended: float32 [16384, 256], P(('pb', 'kv'))
- attended_tangent: float32 [16384, 256], P(('pb', 'kv'))
All inputs are finite; a program needn't handle non-finite values.
Results may differ from a plain program's by a relative error of at most 0.0003.
Values sent between devices are 32-bit elements; how exact they have to be, the bound alone decides.
A program may use at most 128 MiB of HBM per device.

v0:
```python
import math

import jax
import jax.numpy as jnp
from jax import lax
from jax.sharding import PartitionSpec as P

DH = 128


def merged(value, axis, join):
    pieces = jax.tree.map(lambda part: lax.all_gather(part, axis), value)
    head = jax.tree.map(lambda part: part[0], pieces)
    tail = jax.tree.map(lambda part: part[1:], pieces)
    running, _ = lax.scan(lambda running, slab: (join(running, slab), None), head, tail)
    return running


def cross(left, right):
    return lax.dot_general(
        left,
        right,
        (((1,), (1,)), ((), ())),
        precision=lax.Precision.HIGHEST,
        preferred_element_type=jnp.float32,
    )


def product(left, right):
    return jnp.dot(left, right, precision=lax.Precision.HIGHEST, preferred_element_type=jnp.float32)


def widen(factor):
    return jnp.repeat(factor, DH, axis=1)


def combine_parts(first, second):
    peak = jnp.maximum(first[0], second[0])
    scale_a = jnp.exp(first[0] - peak)
    scale_b = jnp.exp(second[0] - peak)
    wide_a = widen(scale_a)
    wide_b = widen(scale_b)
    return (
        peak,
        scale_a * first[1] + scale_b * second[1],
        scale_a * first[2] + scale_b * second[2],
        wide_a * first[3] + wide_b * second[3],
        wide_a * first[4] + wide_b * second[4],
    )


def finish(total, total_t, numer, numer_t):
    attended = numer / widen(total)
    tangent = (numer_t - attended * widen(total_t)) / widen(total)
    return (attended, tangent)


def per_device(queries, keys, values, query_tangent, key_tangent, value_tangent):
    tok_rows = queries.shape[0]
    heads = queries.shape[1] // DH
    scale = 1.0 / math.sqrt(DH)
    block_q, block_dq = (
        lax.all_gather(queries, "kv", axis=0, tiled=True),
        lax.all_gather(query_tangent, "kv", axis=0, tiled=True),
    )
    q_count = block_q.shape[0]
    peak = jnp.full((q_count, heads), -1e30, jnp.float32)
    key_p = lax.all_gather(keys, "pb", axis=0, tiled=True)
    val_p = lax.all_gather(values, "pb", axis=0, tiled=True)
    dkey_p = lax.all_gather(key_tangent, "pb", axis=0, tiled=True)
    dval_p = lax.all_gather(value_tangent, "pb", axis=0, tiled=True)
    peaks = []
    totals = []
    totals_t = []
    numers = []
    numers_t = []
    for head in range(heads):
        cols = slice(head * DH, (head + 1) * DH)
        q_h = block_q[:, cols]
        k_h = key_p[:, cols]
        scores = cross(q_h, k_h) * scale
        score_t = (cross(block_dq[:, cols], k_h) + cross(q_h, dkey_p[:, cols])) * scale
        old = peak[:, head]
        fresh = jnp.maximum(old, jnp.max(scores, axis=1))
        expo = jnp.exp(scores - fresh[:, None])
        weighted = expo * score_t
        peaks.append(fresh)
        totals.append(jnp.sum(expo, axis=1))
        totals_t.append(jnp.sum(weighted, axis=1))
        numers.append(product(expo, val_p[:, cols]))
        numers_t.append(product(weighted, val_p[:, cols]) + product(expo, dval_p[:, cols]))
    peak = jnp.stack(peaks, axis=1)
    total = jnp.stack(totals, axis=1)
    total_t = jnp.stack(totals_t, axis=1)
    numer = jnp.concatenate(numers, axis=1)
    numer_t = jnp.concatenate(numers_t, axis=1)
    joined = merged((peak, total, total_t, numer, numer_t), "kv", combine_parts)
    offset = lax.axis_index("kv") * tok_rows
    own = [lax.dynamic_slice_in_dim(item, offset, tok_rows, 0) for item in joined[1:]]
    return finish(own[0], own[1], own[2], own[3])


def solution(mesh):
    in_specs = (
        P(("pb", "kv"), None),
        P(("pb", "kv"), None),
        P(("pb", "kv"), None),
        P(("pb", "kv"), None),
        P(("pb", "kv"), None),
        P(("pb", "kv"), None),
    )
    out_specs = (P(("pb", "kv"), None), P(("pb", "kv"), None))
    return jax.shard_map(
        per_device, mesh=mesh, in_specs=in_specs, out_specs=out_specs, check_vma=False
    )
```

profile of v0, /device:TPU:0, one launch (start us, length us, event | category | flops | bytes accessed | tf_op | source)
XLA Modules:
  0.0 530.7 jit_solution(8780121762548247383)
XLA Ops:
  11.2 48.9 %all-gather.14.cloned.1.call-done = f32[1024,256]{1,0:T(8,128)} async-done(((f32[128,256]{1,0:T(8,128)}), f32[1024,256]{1,0:T(8,128)}) %all-gather.14.cloned.1.call-update) | async-done | bytes 1048592 | tf_op jit(solution)/shard_map/all_gather | solution.py:63
  60.0 34.3 %all-gather.16.cloned.1.call-done = f32[2048,256]{1,0:T(8,128)} async-done(((f32[128,256]{1,0:T(8,128)}), f32[2048,256]{1,0:T(8,128)}) %all-gather.16.cloned.1.call-update) | async-done | bytes 2097168 | tf_op jit(solution)/shard_map/all_gather | solution.py:68
  94.3 10.4 %multiply_reduce_fusion = (f32[1024]{0:T(1024)S(1)}, f32[1024,2048]{1,0:T(8,128)}) fusion(f32[2048,256]{1,0:T(8,128)} %all-gather.16.cloned.1.call-done, f32[1024,256]{1,0:T(8,128)} %all-gather.14.cloned.1.call-done), kind=kOutput, calls=%fused_computation.18 | convolution fusion | flops 3225418752 | bytes 9965568 | tf_op jit(solution)/shard_map/dot_general | solution.py:20
  104.8 9.2 %multiply_reduce_fusion.1 = (f32[1024]{0:T(1024)S(1)}, f32[1024,2048]{1,0:T(8,128)}) fusion(f32[2048,256]{1,0:T(8,128)S(1)} %copy-done.3, f32[1024,256]{1,0:T(8,128)S(1)} %copy-done.4), kind=kOutput, calls=%fused_computation.19 | convolution fusion | flops 3225418752 | bytes 9965568 | tf_op jit(solution)/shard_map/dot_general | solution.py:20
  114.0 16.0 %all-gather.22.cloned.1.call-done = f32[2048,256]{1,0:T(8,128)} async-done(((f32[128,256]{1,0:T(8,128)}), f32[2048,256]{1,0:T(8,128)}) %all-gather.22.cloned.1.call-update) | async-done | bytes 2097168 | tf_op jit(solution)/shard_map/all_gather | solution.py:69
  130.0 13.1 %fusion.11 = f32[1024,128]{0,1:T(8,128)S(1)} fusion(f32[2048,256]{1,0:T(8,128)} %all-gather.22.cloned.1.call-done, f32[1024,2048]{1,0:T(8,128)} %get-tuple-element.119, f32[1024]{0:T(1024)S(1)} %broadcast_maximum_fusion), kind=kOutput, calls=%fused_computation.30 | convolution fusion | flops 3225419776 | bytes 9965568 | tf_op jit(solution)/shard_map/dot_general | solution.py:30
  143.1 11.3 %fusion.15 = f32[1024,128]{0,1:T(8,128)S(1)} fusion(f32[2048,256]{1,0:T(8,128)} %all-gather.22.cloned.1.call-done, f32[1024,2048]{1,0:T(8,128)S(1)} %copy-done, f32[1024]{0:T(1024)S(1)} %broadcast_maximum_fusion.1), kind=kOutput, calls=%fused_computation.34 | convolution fusion | flops 3225419776 | bytes 9965568 | tf_op jit(solution)/shard_map/dot_general | solution.py:30
  155.4 24.0 %all-gather.18.cloned.1.call-done = f32[1024,256]{1,0:T(8,128)} async-done(((f32[128,256]{1,0:T(8,128)}), f32[1024,256]{1,0:T(8,128)}) %all-gather.18.cloned.1.call-update) | async-done | bytes 1048592 | tf_op jit(solution)/shard_map/all_gather | solution.py:64
  179.4 10.2 %fusion.17 = f32[1024,2048]{1,0:T(8,128)} fusion(f32[2048,256]{1,0:T(8,128)S(1)} %copy-done.3, f32[1024,256]{1,0:T(8,128)} %all-gather.18.cloned.1.call-done), kind=kOutput, calls=%fused_computation.36 | convolution fusion | flops 3221225472 | bytes 9961472 | tf_op jit(solution)/shard_map/dot_general | solution.py:20
  189.7 8.8 %fusion.21 = f32[1024,2048]{1,0:T(8,128)} fusion(f32[2048,256]{1,0:T(8,128)S(1)} %copy-done.3, f32[1024,256]{1,0:T(8,128)S(1)} %copy-done.5), kind=kOutput, calls=%fused_computation.40 | convolution fusion | flops 3221225472 | bytes 9961472 | tf_op jit(solution)/shard_map/dot_general | solution.py:20
  198.5 15.1 %all-gather.20.cloned.1.call-done = f32[2048,256]{1,0:T(8,128)} async-done(((f32[128,256]{1,0:T(8,128)}), f32[2048,256]{1,0:T(8,128)}) %all-gather.20.cloned.1.call-update) | async-done | bytes 2097168 | tf_op jit(solution)/shard_map/all_gather | solution.py:70
  213.6 13.0 %fusion.36 = (f32[1024]{0:T(1024)S(1)}, f32[1024,2048]{1,0:T(8,128)S(1)}) fusion(f32[1024,2048]{1,0:T(8,128)} %fusion.17, f32[2048,256]{1,0:T(8,128)} %all-gather.20.cloned.1.call-done, f32[1024,256]{1,0:T(8,128)S(1)} %copy-done.4, f32[1024]{0:T(1024)S(1)} %broadcast_maximum_fusion, f32[1024,2048]{1,0:T(8,128)} %get-tuple-element.119), kind=kOutput, calls=%fused_computation.63 | convolution fusion | flops 3233807360 | bytes 26746880 | tf_op jit(solution)/shard_map/dot_general | solution.py:20
  226.6 9.7 %fusion.9 = f32[1024,128]{0,1:T(8,128)} fusion(f32[1024,2048]{1,0:T(8,128)S(1)} %get-tuple-element.123, f32[2048,256]{1,0:T(8,128)S(1)} %copy-done.2), kind=kOutput, calls=%fused_computation.28 | convolution fusion | flops 3221225472 | bytes 9961472 | tf_op jit(solution)/shard_map/dot_general | solution.py:30
  236.3 11.2 %fusion.37 = (f32[1024]{0:T(1024)S(1)}, f32[1024,2048]{1,0:T(8,128)S(1)}) fusion(f32[1024,2048]{1,0:T(8,128)S(1)} %copy-done.1, f32[2048,256]{1,0:T(8,128)S(1)} %copy-done.7, f32[1024,256]{1,0:T(8,128)S(1)} %copy-done.4, f32[1024]{0:T(1024)S(1)} %broadcast_maximum_fusion.1, f32[1024,2048]{1,0:T(8,128)} %get-tuple-element.121), kind=kOutput, calls=%fused_computation.64 | convolution fusion | flops 3233807360 | bytes 26746880 | tf_op jit(solution)/shard_map/dot_general | solution.py:20
  247.6 8.9 %fusion.13 = f32[1024,128]{0,1:T(8,128)S(1)} fusion(f32[1024,2048]{1,0:T(8,128)S(1)} %get-tuple-element.125, f32[2048,256]{1,0:T(8,128)S(1)} %copy-done.2), kind=kOutput, calls=%fused_computation.32 | convolution fusion | flops 3221225472 | bytes 9961472 | tf_op jit(solution)/shard_map/dot_general | solution.py:30
  256.5 12.0 %convolution_add_fusion = f32[1024,128]{0,1:T(8,128)S(1)} fusion(f32[1024,128]{0,1:T(8,128)S(1)} %copy-done.8, f32[2048,256]{1,0:T(8,128)} %all-gather.24.cloned.1.call-done, f32[1024,2048]{1,0:T(8,128)} %get-tuple-element.119, f32[1024]{0:T(1024)S(1)} %broadcast_maximum_fusion), kind=kOutput, calls=%fused_computation.20 | convolution fusion | flops 3225550848 | bytes 10489856 | tf_op jit(solution)/shard_map/dot_general | solution.py:30
  268.5 11.9 %convolution_add_fusion.1 = f32[1024,128]{0,1:T(8,128)S(1)} fusion(f32[1024,128]{0,1:T(8,128)S(1)} %fusion.13, f32[2048,256]{1,0:T(8,128)S(1)} %copy-done.6, f32[1024,2048]{1,0:T(8,128)} %get-tuple-element.121, f32[1024]{0:T(1024)S(1)} %broadcast_maximum_fusion.1), kind=kOutput, calls=%fused_computation.21 | convolution fusion | flops 3225550848 | bytes 10489856 | tf_op jit(solution)/shard_map/dot_general | solution.py:30
  281.5 34.8 %all-gather = f32[8192,2]{0,1:T(2,128)S(1)} all-gather(f32[1024,2]{0,1:T(2,128)S(1)} %pad_maximum_fusion.2), channel_id=2, replica_groups=mesh['pb'=16,'kv'=8] {'kv'}, dimensions={0}, use_global_device_ids=true | all-gather | bytes 73728 | tf_op jit(solution)/shard_map/all_gather | solution.py:12
  316.3 7.5 %fusion.33 = (f32[1024]{0:T(1024)S(1)}, f32[1024]{0:T(1024)S(1)}) fusion(f32[1024]{0:T(1024)S(1)} %broadcast_maximum_fusion.1, f32[1024,2048]{1,0:T(8,128)} %get-tuple-element.121, f32[1024]{0:T(1024)S(1)} %broadcast_maximum_fusion, f32[1024,2048]{1,0:T(8,128)} %get-tuple-element.119), kind=kLoop, calls=%fused_computation.61 | loop fusion | flops 12580864 | bytes 16793600 | tf_op jit(solution)/shard_map/reduce_sum | solution.py:88
  323.8 34.7 %all-gather.1 = f32[8192,2]{0,1:T(2,128)S(1)} all-gather(f32[1024,2]{0,1:T(2,128)S(1)} %pad_maximum_fusion.3), channel_id=3, replica_groups=mesh['pb'=16,'kv'=8] {'kv'}, dimensions={0}, use_global_device_ids=true | all-gather | bytes 73728 | tf_op jit(solution)/shard_map/all_gather | solution.py:12
  358.5 34.6 %all-gather.2 = f32[8192,2]{0,1:T(2,128)S(1)} all-gather(f32[1024,2]{0,1:T(2,128)S(1)} %pad_maximum_fusion.4), channel_id=4, replica_groups=mesh['pb'=16,'kv'=8] {'kv'}, dimensions={0}, use_global_device_ids=true | all-gather | bytes 73728 | tf_op jit(solution)/shard_map/all_gather | solution.py:12
  393.1 6.8 %slice.120 = f32[7168,256]{0,1:T(8,128)} slice(f32[8192,256]{0,1:T(8,128)} %all-gather.26.cloned.1.call-done), slice={[1024:8192], [0:256]} | slice | bytes 14680064 | tf_op jit(solution)/shard_map/slice | solution.py:14
  399.9 8.6 %copy.18 = f32[7168,256]{1,0:T(8,128)} copy(f32[7168,256]{0,1:T(8,128)} %slice.120) | data formatting | bytes 14680064 | tf_op jit(solution)/shard_map/slice | solution.py:14
  408.9 60.7 %all-gather.28.cloned.1.call-done = f32[8192,256]{0,1:T(8,128)} async-done(((f32[1024,256]{0,1:T(8,128)}), f32[8192,256]{0,1:T(8,128)}) %all-gather.28.cloned.1.call-update) | async-done | bytes 8388624 | tf_op jit(solution)/shard_map/all_gather | solution.py:12
  469.6 6.8 %slice.121 = f32[7168,256]{0,1:T(8,128)} slice(f32[8192,256]{0,1:T(8,128)} %all-gather.28.cloned.1.call-done), slice={[1024:8192], [0:256]} | slice | bytes 14680064 | tf_op jit(solution)/shard_map/slice | solution.py:14
  476.4 8.4 %copy.19 = f32[7168,256]{1,0:T(8,128)} copy(f32[7168,256]{0,1:T(8,128)} %slice.121) | data formatting | bytes 14680064 | tf_op jit(solution)/shard_map/slice | solution.py:14
  485.2 36.8 %while.18 = (s32[]{:T(128)}, f32[1024,2]{0,1:T(2,128)S(1)}, f32[1024,2]{0,1:T(2,128)S(1)}, f32[1024,2]{0,1:T(2,128)S(1)}, f32[1024,256]{1,0:T(8,128)S(1)}, /*ind...) while((s32[]{:T(128)}, f32[1024,2]{0,1:T(2,128)S(1)}, ...), condition=%wide.region_7.8_spmd, body=%wide.region_6.7_spmd.sunk | while | flops 1591298 | bytes 10641545 | solution.py:15
  488.3 2.2 fusion.45
  493.5 2.2 fusion.45
  498.8 2.2 fusion.45
  509.3 2.2 fusion.45
  519.8 2.2 fusion.45
  (115 shorter events, 33.5 us)
Async XLA Ops:
  7.2 52.9 %all-gather.14.cloned.1.call-start = ((), (), s32[]{:S(2)}) async-start(), calls=%async_computation | async-start | bytes 1179648 | tf_op jit(solution)/shard_map/all_gather | solution.py:63
  7.9 86.5 %all-gather.16.cloned.1.call-start = ((), (), s32[]{:S(2)}) async-start(), calls=%async_computation.1 | async-start | bytes 2228224 | tf_op jit(solution)/shard_map/all_gather | solution.py:68
  8.6 121.3 %all-gather.22.cloned.1.call-start = ((), (), s32[]{:S(2)}) async-start(), calls=%async_computation.4 | async-start | bytes 2228224 | tf_op jit(solution)/shard_map/all_gather | solution.py:69
  9.4 170.1 %all-gather.18.cloned.1.call-start = ((), (), s32[]{:S(2)}) async-start(), calls=%async_computation.2 | async-start | bytes 1179648 | tf_op jit(solution)/shard_map/all_gather | solution.py:64
  10.0 203.6 %all-gather.20.cloned.1.call-start = ((), (), s32[]{:S(2)}) async-start(), calls=%async_computation.3 | async-start | bytes 2228224 | tf_op jit(solution)/shard_map/all_gather | solution.py:70
  10.5 245.9 %all-gather.24.cloned.1.call-start = ((), (), s32[]{:S(2)}) async-start(), calls=%async_computation.5 | async-start | bytes 2228224 | tf_op jit(solution)/shard_map/all_gather | solution.py:71
  11.1 382.0 %all-gather.26.cloned.1.call-start = ((), (), s32[]{:S(2)}) async-start(), calls=%async_computation.6 | async-start | bytes 9437184 | tf_op jit(solution)/shard_map/all_gather | solution.py:12
  60.0 44.8 %copy-start.4 = (f32[1024,256]{1,0:T(8,128)S(1)}, f32[1024,256]{1,0:T(8,128)}, u32[]{:S(2)}) copy-start(f32[1024,256]{1,0:T(8,128)} %all-gather.14.cloned.1.call-done) | copy-start | bytes 3145732
  94.3 10.5 %copy-start.3 = (f32[2048,256]{1,0:T(8,128)S(1)}, f32[2048,256]{1,0:T(8,128)}, u32[]{:S(2)}) copy-start(f32[2048,256]{1,0:T(8,128)} %all-gather.16.cloned.1.call-done) | copy-start | bytes 6291460
  130.0 13.1 %copy-start = (f32[1024,2048]{1,0:T(8,128)S(1)}, f32[1024,2048]{1,0:T(8,128)}, u32[]{:S(2)}) copy-start(f32[1024,2048]{1,0:T(8,128)} %get-tuple-element.121) | copy-start | bytes 25165828
  155.4 314.2 %all-gather.28.cloned.1.call-start = ((), (), s32[]{:S(2)}) async-start(), calls=%async_computation.7 | async-start | bytes 9437184 | tf_op jit(solution)/shard_map/all_gather | solution.py:12
  179.4 10.2 %copy-start.5 = (f32[1024,256]{1,0:T(8,128)S(1)}, f32[1024,256]{1,0:T(8,128)}, u32[]{:S(2)}) copy-start(f32[1024,256]{1,0:T(8,128)} %all-gather.18.cloned.1.call-done) | copy-start | bytes 3145732
  198.5 28.1 %copy-start.2 = (f32[2048,256]{1,0:T(8,128)S(1)}, f32[2048,256]{1,0:T(8,128)}, u32[]{:S(2)}) copy-start(f32[2048,256]{1,0:T(8,128)} %all-gather.22.cloned.1.call-done) | copy-start | bytes 6291460
  213.6 22.7 %copy-start.7 = (f32[2048,256]{1,0:T(8,128)S(1)}, f32[2048,256]{1,0:T(8,128)}, u32[]{:S(2)}) copy-start(f32[2048,256]{1,0:T(8,128)} %all-gather.20.cloned.1.call-done) | copy-start | bytes 6291460
  226.6 9.7 %copy-start.1 = (f32[1024,2048]{1,0:T(8,128)S(1)}, f32[1024,2048]{1,0:T(8,128)}, u32[]{:S(2)}) copy-start(f32[1024,2048]{1,0:T(8,128)} %fusion.21) | copy-start | bytes 25165828
  247.6 8.9 %copy-start.8 = (f32[1024,128]{0,1:T(8,128)S(1)}, f32[1024,128]{0,1:T(8,128)}, u32[]{:S(2)}) copy-start(f32[1024,128]{0,1:T(8,128)} %fusion.9) | copy-start | bytes 1572868
  256.5 12.0 %copy-start.6 = (f32[2048,256]{1,0:T(8,128)S(1)}, f32[2048,256]{1,0:T(8,128)}, u32[]{:S(2)}) copy-start(f32[2048,256]{1,0:T(8,128)} %all-gather.24.cloned.1.call-done) | copy-start | bytes 6291460
  316.3 7.5 %copy-start.9 = (f32[8192,2]{0,1:T(2,128)}, f32[8192,2]{0,1:T(2,128)S(1)}, u32[]{:S(2)}) copy-start(f32[8192,2]{0,1:T(2,128)S(1)} %all-gather) | copy-start | bytes 196612
  358.5 50.1 %copy-start.10 = (f32[8192,2]{0,1:T(2,128)}, f32[8192,2]{0,1:T(2,128)S(1)}, u32[]{:S(2)}) copy-start(f32[8192,2]{0,1:T(2,128)S(1)} %all-gather.1) | copy-start | bytes 196612
  393.1 15.5 %copy-start.11 = (f32[8192,2]{0,1:T(2,128)}, f32[8192,2]{0,1:T(2,128)S(1)}, u32[]{:S(2)}) copy-start(f32[8192,2]{0,1:T(2,128)S(1)} %all-gather.2) | copy-start | bytes 196612
  399.9 8.6 %slice-start = ((f32[8192,256]{0,1:T(8,128)}), f32[1024,256]{0,1:T(8,128)S(1)}, s32[]{:S(2)}) async-start(f32[8192,256]{0,1:T(8,128)} %all-gather.26.cloned.1.call-done), calls=%async_computation.8 | async-start | bytes 2097152 | tf_op jit(solution)/shard_map/slice | solution.py:13
  476.4 8.5 %slice-start.1 = ((f32[8192,256]{0,1:T(8,128)}), f32[1024,256]{0,1:T(8,128)S(1)}, s32[]{:S(2)}) async-start(f32[8192,256]{0,1:T(8,128)} %all-gather.28.cloned.1.call-done), calls=%async_computation.9 | async-start | bytes 2097152 | tf_op jit(solution)/shard_map/slice | solution.py:13
  476.4 8.8 %slice-start.2 = ((f32[8192,2]{0,1:T(2,128)}), f32[7168,2]{0,1:T(2,128)S(1)}, s32[]{:S(2)}) async-start(f32[8192,2]{0,1:T(2,128)} %copy-done.9), calls=%async_computation.10 | async-start | bytes 114688 | tf_op jit(solution)/shard_map/slice | solution.py:14
  476.4 8.8 %slice-start.3 = ((f32[8192,2]{0,1:T(2,128)}), f32[7168,2]{0,1:T(2,128)S(1)}, s32[]{:S(2)}) async-start(f32[8192,2]{0,1:T(2,128)} %copy-done.10), calls=%async_computation.11 | async-start | bytes 114688 | tf_op jit(solution)/shard_map/slice | solution.py:14
  476.4 8.8 %slice-start.4 = ((f32[8192,2]{0,1:T(2,128)}), f32[7168,2]{0,1:T(2,128)S(1)}, s32[]{:S(2)}) async-start(f32[8192,2]{0,1:T(2,128)} %copy-done.11), calls=%async_computation.12 | async-start | bytes 114688 | tf_op jit(solution)/shard_map/slice | solution.py:14
Sparse Core Ops, SparseCore 0:
  10.3 49.6 all-gather.13
  61.7 32.5 all-gather.15
  96.1 33.8 all-gather.21
  132.1 47.2 all-gather.17
  181.0 32.5 all-gather.19
  215.2 33.8 all-gather.23
  251.4 109.4 all-gather.25
  363.3 106.2 all-gather.27
where the time goes:
time: 540 us; the launch traced here: 531 us
  waiting for transfers between devices  203 us (38%)
  matrix products  130 us (24%)
  blocking collectives  104 us (19%)
  local copies, waits for them, and re-layouts  52.5 us (10%)
  other arithmetic  26.4 us (5%)
  between operations  14.8 us (3%)
    all_gather x3, blocking collectives, merged(): pieces = jax.tree.map(lambda part: lax.all_gather(part, axis), value)  104 us
    dot_general x6, matrix products, product(): jnp.dot(left, right, precision=lax.Precision.HIGHEST, preferred_element_t...  66.8 us
    dot_general x6, matrix products, cross(): lax.dot_general(left, right, (((1,), (1,)), ((), ())), precision=lax.Prec...  62.9 us
    all_gather x2, waiting for transfers between devices, merged(): pieces = jax.tree.map(lambda part: lax.all_gather(part, axis), value)  60.7 us
    all_gather x1, waiting for transfers between devices, per_device(): lax.all_gather(queries, 'kv', axis=0, tiled=True)  48.9 us
    all_gather x1, waiting for transfers between devices, per_device(): key_p = lax.all_gather(keys, 'pb', axis=0, tiled=True)  34.3 us
    slice x10, local copies, waits for them, and re-layouts, merged(): tail = jax.tree.map(lambda part: part[1:], pieces)  30.7 us
    all_gather x1, waiting for transfers between devices, per_device(): lax.all_gather(query_tangent, 'kv', axis=0, tiled=True)  24 us
  transfers between devices with their start and end apart: 8, of which 6 were waited for; matrix products, arithmetic and copies ran while one was open for 29% of the time, Pallas kernels for 0%

commit v1 on v0

v1 whole, which is shorter than its diff:
```python
import math

import jax
import jax.numpy as jnp
from jax import lax
from jax.experimental import pallas as pl
from jax.experimental.pallas import tpu as pltpu
from jax.sharding import PartitionSpec as P

DH = 128
LN = 256
F32, BF = jnp.float32, jnp.bfloat16
MESH = pl.DeviceIdType.MESH
ORDER = (0, 1, 2, 4, 3, 5, 6, 7)
POS = tuple(ORDER.index(r) for r in range(8))
THIRD = ((0, 88), (88, 88), (176, 80))
PART = ((0, 96), (96, 96), (192, 88))
STAT = (88, 184, 272)


def nt(a, b):
    return lax.dot_general(a, b, (((1,), (1,)), ((), ())), preferred_element_type=F32)


def nn(a, b):
    return jnp.dot(a, b, preferred_element_type=F32)


def two(x):
    hi = x.astype(BF)
    return hi, (x - hi.astype(F32)).astype(BF)


def three(x):
    hi = x.astype(BF)
    rest = x - hi.astype(F32)
    mid = rest.astype(BF)
    return hi, mid, (rest - mid.astype(F32)).astype(BF)


def kernel(q, dq, k, dk, v, dv, o, ot, kvb, qb, ks, ky, vh, vl, qs, qx, ac, rb, fin,
           swap_s, swap_r, own_s, ks_s, ks_r, qs_s, qs_r, b_s, b_r, f_s, f_r, f_o):
    pb, kv = lax.axis_index("pb"), lax.axis_index("kv")
    core, x = pb % 2, pb // 4
    z, y = (kv // 4) * 2 + (pb // 2) % 2, kv % 4

    def dev(x, y, z, c):
        return (x * 4 + (z % 2) * 2 + c, (z // 2) * 4 + y)

    def near(i):
        return i + 1 - 2 * (i % 2)

    def far(i):
        return (i + 2 * (i % 2) + 3) % 4

    kn = (dev(near(x), y, z, core), dev(x, near(y), z, core), dev(x, y, near(z), core))
    qn = (dev(far(x), y, z, core), dev(x, far(y), z, core), dev(x, y, far(z), core))
    sib = dev(x, y, z, 1 - core)

    barrier = pltpu.get_barrier_semaphore()
    for other in kn + qn + (sib,):
        pl.semaphore_signal(barrier, inc=1, device_id=other, device_id_type=MESH)
    pl.semaphore_wait(barrier, 7)

    mine = pl.ds(pl.multiple_of(core * DH, DH), DH)
    theirs = pl.ds(pl.multiple_of((1 - core) * DH, DH), DH)
    rows = pl.ds(pl.multiple_of(core * 128, 128), 128)
    swaps, owns = [], []
    for i, (ref, dst, a) in enumerate(
        ((q, qb, 0), (dq, qb, 1), (k, kvb, 0), (dk, kvb, 1), (v, kvb, 2), (dv, kvb, 3))
    ):
        swaps.append(pltpu.make_async_remote_copy(
            src_ref=ref.at[:, theirs], dst_ref=dst.at[a, 0, rows],
            send_sem=swap_s.at[i], recv_sem=swap_r.at[i], device_id=sib, device_id_type=MESH))
        owns.append(pltpu.make_async_copy(ref.at[:, mine], dst.at[a, 0, rows], own_s.at[i]))
    for c in swaps + owns:
        c.start()

    def route(buf, near_of, send, recv):
        def msg(t, to):
            dims = [(t + i) % 3 for i in range(3)]
            d = [i for i in dims if to >> i & 1][-1]
            part = pl.ds(*THIRD[t])
            return pltpu.make_async_remote_copy(
                src_ref=buf.at[:, POS[to ^ (1 << d)], part], dst_ref=buf.at[:, POS[to], part],
                send_sem=send.at[t * 8 + to], recv_sem=recv.at[t * 8 + to],
                device_id=near_of[d], device_id_type=MESH)
        return {(t, to): msg(t, to) for t in range(3) for to in range(1, 8)}

    kmsg, qmsg = route(kvb, kn, ks_s, ks_r), route(qb, qn, qs_s, qs_r)

    def names(t):
        return 1 << t, 1 << (t + 1) % 3, 1 << (t + 2) % 3

    def begin(m):
        for step in range(3):
            for t in range(3):
                m[t, names(t)[step]].start()

    def pass_first(m):
        for t in range(3):
            a, b, c = names(t)
            m[t, a].wait_recv()
            m[t, a | b].start()
            m[t, a | c].start()

    def pass_second(m):
        for t in range(3):
            a, b, c = names(t)
            m[t, b].wait_recv()
            m[t, b | c].start()

    def pass_both(m):
        for t in range(3):
            a, b, c = names(t)
            m[t, a | b].wait_recv()
            m[t, a | b | c].start()

    def end_near(m):
        for t in range(3):
            m[t, names(t)[2]].wait_recv()

    def end_far(m):
        for t in range(3):
            a, b, c = names(t)
            for to in (a | c, b | c, a | b | c):
                m[t, to].wait_recv()

    root = 1.0 / math.sqrt(DH)
    base2 = root * math.log2(math.e)

    def prep_k(first, count):
        def one(i, _):
            r = pl.ds(pl.multiple_of(i * LN, LN), LN)
            kh, km, kl = three(kvb[0, i])
            dh, dm = two(kvb[1, i])
            ks[r, :] = jnp.concatenate([kh, km, kh, km, kl, kh], axis=1)
            ky[r, :] = jnp.concatenate([kh, dh, km, dm, kh, dh], axis=1)
            for a in range(2):
                hi, lo = two(jnp.transpose(kvb[2 + a, i]))
                vh[a * DH:(a + 1) * DH, r] = hi
                vl[a * DH:(a + 1) * DH, r] = lo
            return 0
        lax.fori_loop(first, first + count, one, 0)

    def prep_q(first, count):
        def one(i, _):
            r = pl.ds(pl.multiple_of(i * LN, LN), LN)
            raw = qb[0, i]
            h, m, l = three(raw * base2)
            qs[r, :] = jnp.concatenate([h, h, m, m, h, l], axis=1)
            h, m = two(raw * root)
            dh, dm = two(qb[1, i] * root)
            qx[r, :] = jnp.concatenate([dh, h, dh, h, dm, m], axis=1)
            ac[i] = jnp.zeros(ac.shape[1:], F32)
            ac[i, 88:89, :] = jnp.full((1, LN), -1e30, F32)
            return 0
        lax.fori_loop(first, first + count, one, 0)

    def tile(first, count, k0, keys):
        r = pl.ds(pl.multiple_of(first * LN, LN), count * LN)
        c = slice(k0 * LN, k0 * LN + keys)

        def lanes(row):
            return jnp.concatenate([ac[first + i, row:row + 1, :] for i in range(count)], axis=1)

        s = nt(ks[c, :], qs[r, :])
        t = nt(ky[c, :], qx[r, :])
        old = lanes(88)
        peak = jnp.maximum(old, jnp.max(s, axis=0, keepdims=True))
        fade = jnp.exp2(old - peak)
        e = jnp.exp2(s - peak)
        w = e * t
        total = lanes(89) * fade + jnp.sum(e, axis=0, keepdims=True)
        total_t = lanes(90) * fade + jnp.sum(w, axis=0, keepdims=True)
        eh, el = two(e)
        wh, wl = two(w)
        hi, lo = vh[:, c], vl[:, c]
        n = nn(hi, eh) + nn(lo, eh) + nn(hi, el)
        u = nn(hi[:DH], wh) + nn(lo[:DH], wh) + nn(hi[:DH], wl)
        tan = n[DH:] + u
        for i in range(count):
            s_ = slice(i * LN, (i + 1) * LN)
            f = fade[:, s_]
            at = first + i
            ac[at, 0:88, :] = ac[at, 0:88, :] * f + n[0:88, s_]
            ac[at, 96:136, :] = ac[at, 96:136, :] * f + n[88:128, s_]
            ac[at, 136:184, :] = ac[at, 136:184, :] * f + tan[0:48, s_]
            ac[at, 192:272, :] = ac[at, 192:272, :] * f + tan[48:128, s_]
            ac[at, 88:89, :] = peak[:, s_]
            ac[at, 89:90, :] = total[:, s_]
            ac[at, 90:91, :] = total_t[:, s_]

    def sweep(first, tiles, count, k0, keys):
        def one(i, _):
            tile(first + i * count, count, k0, keys)
            return 0
        lax.fori_loop(0, tiles, one, 0)

    def bmsg(t, src, d, i, n_):
        r0, n = PART[t]
        return pltpu.make_async_remote_copy(
            src_ref=ac.at[POS[src], pl.ds(r0, n)], dst_ref=rb.at[t, i, pl.ds(0, n)],
            send_sem=b_s.at[t * 7 + i], recv_sem=b_r.at[t * 7 + i],
            device_id=qn[d], device_id_type=MESH)

    back = {}
    for t in range(3):
        a, b, c = names(t)
        for i, to in enumerate((0, a, b, a | b)):
            back[t, 1, to] = bmsg(t, to | c, (t + 2) % 3, i, 0)
        for i, to in enumerate((0, a)):
            back[t, 2, to] = bmsg(t, to | b, (t + 1) % 3, 4 + i, 0)
        back[t, 3, 0] = bmsg(t, a, t, 6, 0)

    def leave(pos):
        ac[pos, 184:192, :] = ac[pos, 88:96, :]
        ac[pos, 272:280, :] = ac[pos, 88:96, :]
        r = ORDER[pos]
        for t in range(3):
            c = names(t)[2]
            if r & c:
                back[t, 1, r ^ c].start()

    def merge(t, step, to):
        back[t, step, to].wait_recv()
        a, b, _ = names(t)
        i = {1: {0: 0, a: 1, b: 2, a | b: 3}, 2: {0: 4, a: 5}, 3: {0: 6}}[step][to]
        r0, n = PART[t]
        st, p = STAT[t], POS[to]
        m1, m2 = ac[p, st:st + 1, :], rb[t, i, n - 8:n - 7, :]
        top = jnp.maximum(m1, m2)
        f1, f2 = jnp.exp2(m1 - top), jnp.exp2(m2 - top)
        ac[p, r0:r0 + n, :] = ac[p, r0:r0 + n, :] * f1 + rb[t, i, :n, :] * f2
        ac[p, st:st + 1, :] = top

    for i in range(6):
        swaps[i].wait_recv()
        owns[i].wait()
    begin(qmsg)
    begin(kmsg)
    prep_k(0, 1)
    prep_q(0, 1)
    tile(0, 1, 0, 256)
    pass_first(qmsg)
    pass_first(kmsg)
    pass_second(qmsg)
    end_near(qmsg)
    prep_q(1, 3)
    sweep(1, 1, 3, 0, 256)
    pass_second(kmsg)
    pass_both(qmsg)
    end_near(kmsg)
    prep_k(1, 3)
    sweep(0, 2, 2, 1, 768)
    pass_both(kmsg)
    end_far(qmsg)
    prep_q(4, 4)
    sweep(4, 2, 2, 0, 1024)
    end_far(kmsg)
    prep_k(4, 4)
    for first in (6, 4, 2, 0):
        tile(first, 2, 4, 1024)
        leave(first + 1)
        leave(first)
    for t in range(3):
        a, b, c = names(t)
        merge(t, 1, a | b)
        back[t, 2, a].start()
        merge(t, 1, b)
        back[t, 2, 0].start()
    for t in range(3):
        a, b, c = names(t)
        merge(t, 1, a)
        merge(t, 2, a)
        back[t, 3, 0].start()
    for t in range(3):
        merge(t, 1, 0)
        merge(t, 2, 0)
    for t in range(3):
        merge(t, 3, 0)

    inv = [1.0 / ac[0, s + 1:s + 2, :] for s in STAT]
    rt = [ac[0, s + 2:s + 3, :] for s in STAT]
    att = jnp.concatenate([ac[0, 0:88, :] * inv[0], ac[0, 96:136, :] * inv[1]], axis=0)
    tan = jnp.concatenate([
        (ac[0, 136:184, :] - att[0:48] * rt[1]) * inv[1],
        (ac[0, 192:272, :] - att[48:128] * rt[2]) * inv[2],
    ], axis=0)
    fin[0] = jnp.transpose(att)
    fin[1] = jnp.transpose(tan)
    away = pl.ds(pl.multiple_of((1 - core) * 128, 128), 128)
    ends = []
    for i, out in enumerate((o, ot)):
        ends.append(pltpu.make_async_remote_copy(
            src_ref=fin.at[i, away], dst_ref=out.at[:, mine],
            send_sem=f_s.at[i], recv_sem=f_r.at[i], device_id=sib, device_id_type=MESH))
        ends.append(pltpu.make_async_copy(fin.at[i, rows], out.at[:, mine], f_o.at[i]))
    for c in ends:
        c.start()
    for c in ends:
        c.wait()
    for c in swaps:
        c.wait_send()
    for m in (kmsg, qmsg, back):
        for c in m.values():
            c.wait_send()


def per_device(queries, keys, values, query_tangent, key_tangent, value_tangent):
    hbm = pl.BlockSpec(memory_space=pl.ANY)
    dma = pltpu.SemaphoreType.DMA
    shape = jax.ShapeDtypeStruct(queries.shape, F32)
    return pl.pallas_call(
        kernel,
        out_shape=(shape, shape),
        in_specs=[hbm] * 6,
        out_specs=(hbm, hbm),
        scratch_shapes=[
            pltpu.VMEM((4, 8, LN, DH), F32),
            pltpu.VMEM((2, 8, LN, DH), F32),
            pltpu.VMEM((2048, 768), BF),
            pltpu.VMEM((2048, 768), BF),
            pltpu.VMEM((256, 2048), BF),
            pltpu.VMEM((256, 2048), BF),
            pltpu.VMEM((2048, 768), BF),
            pltpu.VMEM((2048, 768), BF),
            pltpu.VMEM((8, 280, LN), F32),
            pltpu.VMEM((3, 7, 96, LN), F32),
            pltpu.VMEM((2, LN, DH), F32),
            dma((6,)), dma((6,)), dma((6,)),
            dma((24,)), dma((24,)), dma((24,)), dma((24,)),
            dma((21,)), dma((21,)),
            dma((2,)), dma((2,)), dma((2,)),
        ],
        compiler_params=pltpu.CompilerParams(
            collective_id=0, has_side_effects=True, vmem_limit_bytes=62 << 20
        ),
        name="attention_tangent",
    )(queries, query_tangent, keys, key_tangent, values, value_tangent)


def solution(mesh):
    spec = P(("pb", "kv"), None)
    return jax.shard_map(
        per_device, mesh=mesh, in_specs=(spec,) * 6, out_specs=(spec, spec), check_vma=False
    )
```

time: 540 us -> 69.3 us (0.13)
  the two profiles are of different devices: /device:TPU:0 before, /device:TPU:1 now
where the time goes in v1:
time: 69.3 us; the launch traced here: 69.2 us
  Pallas kernels  66.2 us (96%)
  local copies, waits for them, and re-layouts  2.26 us (3%)
    pallas_call x1, Pallas kernels, per_device(): pl.pallas_call(kernel, out_shape=(shape, shape), in_specs=[hbm] * 6, out_...  66.2 us
    unnamed x4, local copies, waits for them, and re-layouts  2.26 us

profile of v1, /device:TPU:1, one launch (start us, length us, event | category | flops | bytes accessed | tf_op | source)
XLA Modules:
  0.0 69.2 jit_solution(6794829899654051906)
XLA Ops:
  0.6 66.2 %attention_tangent.1 = (f32[128,256]{1,0:T(8,128)}, f32[128,256]{1,0:T(8,128)}) custom-call(f32[128,256]{1,0:T(8,128)} %q.1, f32[128,256]{1,0:T(8,128)} %dq.1, f32[128,256]{1,0:T(8,128)} %k.1, f32[128,256]{1,0:T(8,128)} %dk.1, f32[128,256]{1,0:T(8,128)} %v.1, f32[128,256]{1,0:T(8,128)} %dv.1), custom_call_target="tpu_custom_call" | custom-call | tf_op jit(solution)/shard_map/attention_tangent/pallas_call | solution.py:314
  66.9 0.0 copy-start
  66.9 1.6 %copy.10 = f32[128,256]{1,0:T(8,128)} copy(f32[128,256]{1,0:T(8,128)} %get-tuple-element.4) | data formatting | bytes 262144
  68.5 0.0 copy-done
  68.5 0.7 copy.11
Async XLA Ops:
  66.9 1.6 %copy-start = (f32[128,256]{1,0:T(8,128)S(1)}, f32[128,256]{1,0:T(8,128)}, u32[]{:S(2)}) copy-start(f32[128,256]{1,0:T(8,128)} %get-tuple-element.5) | copy-start | bytes 393220

commit v2 on v1

v2 whole, which is shorter than its diff:
```python
import math

import jax
import jax.numpy as jnp
from jax import lax
from jax.experimental import pallas as pl
from jax.experimental.pallas import tpu as pltpu
from jax.sharding import PartitionSpec as P

DH = 128
LN = 128
F32, BF = jnp.float32, jnp.bfloat16
MESH = pl.DeviceIdType.MESH
ORDER = (0, 1, 2, 4, 3, 5, 6, 7)
POS = tuple(ORDER.index(r) for r in range(8))
THIRD = (((0, 48), (48, 40), (88, 40)), ((0, 40), (40, 48), (88, 40)))
PART = ((0, 96), (96, 96), (192, 88))
STAT = (88, 184, 272)


def nt(a, b):
    return lax.dot_general(a, b, (((1,), (1,)), ((), ())), preferred_element_type=F32)


def nn(a, b):
    return jnp.dot(a, b, preferred_element_type=F32)


def two(x):
    hi = x.astype(BF)
    return hi, (x - hi.astype(F32)).astype(BF)


def three(x):
    hi = x.astype(BF)
    rest = x - hi.astype(F32)
    mid = rest.astype(BF)
    return hi, mid, (rest - mid.astype(F32)).astype(BF)


def kernel(q, dq, k, dk, v, dv, o, ot, kvb, qb, ks, ky, vh, vl, qs, qx, ac, rb, fin,
           swap_s, swap_r, own_s, k_s, k_r, q_s, q_r, s_s, s_r, b_s, b_r, f_s, f_r, f_o):
    pb, kv = lax.axis_index("pb"), lax.axis_index("kv")
    core, x = pb % 2, pb // 4
    z, y = (kv // 4) * 2 + (pb // 2) % 2, kv % 4
    head = ((z + 1) // 2) % 2

    def dev(x, y, z, c):
        return (x * 4 + (z % 2) * 2 + c, (z // 2) * 4 + y)

    def near(i):
        return i + 1 - 2 * (i % 2)

    def far(i):
        return (i + 2 * (i % 2) + 3) % 4

    kn = (dev(near(x), y, z, core), dev(x, near(y), z, core))
    qn = (dev(far(x), y, z, core), dev(x, far(y), z, core), dev(x, y, far(z), core))
    mate = dev(x, y, near(z), core)
    sib = dev(x, y, z, 1 - core)

    barrier = pltpu.get_barrier_semaphore()
    for other in kn + qn + (mate, sib):
        pl.semaphore_signal(barrier, inc=1, device_id=other, device_id_type=MESH)
    mine = pl.ds(pl.multiple_of(head * DH, DH), DH)
    theirs = pl.ds(pl.multiple_of((1 - head) * DH, DH), DH)
    table = ((q, qb, 0), (dq, qb, 1), (k, kvb, 0), (dk, kvb, 1), (v, kvb, 2), (dv, kvb, 3))

    def place(dst, a, wave):
        return dst.at[a, 8 * wave] if dst is qb else dst.at[a, 4 * wave, 0]

    owns = [pltpu.make_async_copy(ref.at[:, mine], place(dst, a, 0), own_s.at[i])
            for i, (ref, dst, a) in enumerate(table)]
    for c in owns:
        c.start()
    pl.semaphore_wait(barrier, 7)
    swaps = [pltpu.make_async_remote_copy(
        src_ref=ref.at[:, theirs], dst_ref=place(dst, a, 1), send_sem=swap_s.at[i],
        recv_sem=swap_r.at[i], device_id=mate, device_id_type=MESH)
        for i, (ref, dst, a) in enumerate(table)]
    for c in swaps:
        c.start()

    def names(t):
        return 1 << t, 1 << (t + 1) % 3, 1 << (t + 2) % 3

    def qroute(w, t, to):
        d = [i for i in ((t + j) % 3 for j in range(3)) if to >> i & 1][-1]
        part = pl.ds(*THIRD[w][t])
        i = w * 24 + t * 8 + to
        return pltpu.make_async_remote_copy(
            src_ref=qb.at[:, 8 * w + POS[to ^ (1 << d)], part],
            dst_ref=qb.at[:, 8 * w + POS[to], part],
            send_sem=q_s.at[i], recv_sem=q_r.at[i], device_id=qn[d], device_id_type=MESH)

    qmsg = [{(t, to): qroute(w, t, to) for t in range(3) for to in range(1, 8)} for w in range(2)]

    def begin(m):
        for step in range(3):
            for t in range(3):
                m[t, names(t)[step]].start()

    def pass_first(m):
        for t in range(3):
            a, b, c = names(t)
            m[t, a].wait_recv()
            m[t, a | b].start()
            m[t, a | c].start()

    def pass_second(m):
        for t in range(3):
            a, b, c = names(t)
            m[t, b].wait_recv()
            m[t, b | c].start()

    def pass_both(m):
        for t in range(3):
            a, b, c = names(t)
            m[t, a | b].wait_recv()
            m[t, a | b | c].start()

    def end_near(m):
        for t in range(3):
            m[t, names(t)[2]].wait_recv()

    def end_far(m):
        for t in range(3):
            a, b, c = names(t)
            for to in (a | c, b | c, a | b | c):
                m[t, to].wait_recv()

    def kroute(w, t, to):
        d = 1 - t if to >> (1 - t) & 1 else t
        part = pl.ds(64 * t, 64)
        i = w * 8 + t * 4 + to
        return pltpu.make_async_remote_copy(
            src_ref=kvb.at[:, 4 * w + (to ^ (1 << d)), 0, part],
            dst_ref=kvb.at[:, 4 * w + to, 0, part],
            send_sem=k_s.at[i], recv_sem=k_r.at[i], device_id=kn[d], device_id_type=MESH)

    kmsg = [{(t, to): kroute(w, t, to) for t in range(2) for to in range(1, 4)} for w in range(2)]
    smsg = [pltpu.make_async_remote_copy(
        src_ref=kvb.at[:, i, 0], dst_ref=kvb.at[:, i, 1], send_sem=s_s.at[i],
        recv_sem=s_r.at[i], device_id=sib, device_id_type=MESH) for i in range(8)]

    def kbegin(w):
        for t in range(2):
            kmsg[w][t, 1 << t].start()
        for t in range(2):
            kmsg[w][t, 2 >> t].start()
        smsg[4 * w].start()

    def kpass(w):
        for t in range(2):
            kmsg[w][t, 1 << t].wait_recv()
            kmsg[w][t, 3].start()

    def knear(w):
        for t in range(2):
            kmsg[w][t, 2 >> t].wait_recv()
        smsg[4 * w + 1].start()
        smsg[4 * w + 2].start()

    def kfar(w):
        for t in range(2):
            kmsg[w][t, 3].wait_recv()
        smsg[4 * w + 3].start()

    root = 1.0 / math.sqrt(DH)
    base2 = root * math.log2(math.e)

    def prep_k(first, count):
        for i in range(first, first + count):
            smsg[i].wait_recv()

        def one(i, _):
            r = pl.ds(pl.multiple_of(i * 256, 256), 256)
            kh, km, kl = three(kvb[0, i].reshape(256, DH))
            dh, dm = two(kvb[1, i].reshape(256, DH))
            ks[r, :] = jnp.concatenate([kh, km, kh, km, kl, kh], axis=1)
            ky[r, :] = jnp.concatenate([kh, dh, km, dm, kh, dh], axis=1)
            for a in range(2):
                hi, lo = two(jnp.transpose(kvb[2 + a, i].reshape(256, DH)))
                vh[a * DH:(a + 1) * DH, r] = hi
                vl[a * DH:(a + 1) * DH, r] = lo
            return 0
        lax.fori_loop(first, first + count, one, 0)

    def prep_q(first, count):
        def one(i, _):
            r = pl.ds(pl.multiple_of(i * LN, LN), LN)
            raw = qb[0, i]
            h, m, l = three(raw * base2)
            qs[r, :] = jnp.concatenate([h, h, m, m, h, l], axis=1)
            h, m = two(raw * root)
            dh, dm = two(qb[1, i] * root)
            qx[r, :] = jnp.concatenate([dh, h, dh, h, dm, m], axis=1)
            ac[i] = jnp.zeros(ac.shape[1:], F32)
            ac[i, 88:89, :] = jnp.full((1, LN), -1e30, F32)
            return 0
        lax.fori_loop(first, first + count, one, 0)

    def tile(at, k0, keys):
        first = at * 4
        r = pl.ds(pl.multiple_of(first * LN, 4 * LN), 4 * LN)
        c = slice(k0 * 256, (k0 + keys) * 256)

        def lanes(row):
            return jnp.concatenate([ac[first + i, row:row + 1, :] for i in range(4)], axis=1)

        s = nt(ks[c, :], qs[r, :])
        t = nt(ky[c, :], qx[r, :])
        old = lanes(88)
        peak = jnp.maximum(old, jnp.max(s, axis=0, keepdims=True))
        fade = jnp.exp2(old - peak)
        e = jnp.exp2(s - peak)
        w = e * t
        total = lanes(89) * fade + jnp.sum(e, axis=0, keepdims=True)
        total_t = lanes(90) * fade + jnp.sum(w, axis=0, keepdims=True)
        eh, el = two(e)
        wh, wl = two(w)
        hi, lo = vh[:, c], vl[:, c]
        n = nn(hi, eh) + nn(lo, eh) + nn(hi, el)
        u = nn(hi[:DH], wh) + nn(lo[:DH], wh) + nn(hi[:DH], wl)
        tan = n[DH:] + u
        for i in range(4):
            s_ = slice(i * LN, (i + 1) * LN)
            f = fade[:, s_]
            p = first + i
            ac[p, 0:88, :] = ac[p, 0:88, :] * f + n[0:88, s_]
            ac[p, 96:136, :] = ac[p, 96:136, :] * f + n[88:128, s_]
            ac[p, 136:184, :] = ac[p, 136:184, :] * f + tan[0:48, s_]
            ac[p, 192:272, :] = ac[p, 192:272, :] * f + tan[48:128, s_]
            ac[p, 88:89, :] = peak[:, s_]
            ac[p, 89:90, :] = total[:, s_]
            ac[p, 90:91, :] = total_t[:, s_]

    def sweep(first, count, k0, keys):
        def one(i, _):
            tile(first + i, k0, keys)
            return 0
        lax.fori_loop(0, count, one, 0)

    def bmsg(w, t, src, d, i):
        r0, n = PART[t]
        j = w * 21 + t * 7 + i
        return pltpu.make_async_remote_copy(
            src_ref=ac.at[8 * w + POS[src], pl.ds(r0, n)], dst_ref=rb.at[w, t, i, pl.ds(0, n)],
            send_sem=b_s.at[j], recv_sem=b_r.at[j], device_id=qn[d], device_id_type=MESH)

    back = {}
    for w in range(2):
        for t in range(3):
            a, b, c = names(t)
            for i, to in enumerate((0, a, b, a | b)):
                back[w, t, 1, to] = bmsg(w, t, to | c, (t + 2) % 3, i)
            for i, to in enumerate((0, a)):
                back[w, t, 2, to] = bmsg(w, t, to | b, (t + 1) % 3, 4 + i)
            back[w, t, 3, 0] = bmsg(w, t, a, t, 6)

    def leave(at):
        for p in range(at * 4 + 3, at * 4 - 1, -1):
            ac[p, 184:192, :] = ac[p, 88:96, :]
            ac[p, 272:280, :] = ac[p, 88:96, :]
            w, r = p // 8, ORDER[p % 8]
            for t in range(3):
                c = names(t)[2]
                if r & c:
                    back[w, t, 1, r ^ c].start()

    def merge(w, t, step, to):
        back[w, t, step, to].wait_recv()
        a, b, _ = names(t)
        i = {1: {0: 0, a: 1, b: 2, a | b: 3}, 2: {0: 4, a: 5}, 3: {0: 6}}[step][to]
        r0, n = PART[t]
        st, p = STAT[t], 8 * w + POS[to]
        m1, m2 = ac[p, st:st + 1, :], rb[w, t, i, n - 8:n - 7, :]
        top = jnp.maximum(m1, m2)
        f1, f2 = jnp.exp2(m1 - top), jnp.exp2(m2 - top)
        ac[p, r0:r0 + n, :] = ac[p, r0:r0 + n, :] * f1 + rb[w, t, i, :n, :] * f2
        ac[p, st:st + 1, :] = top

    def back_one(w):
        for t in range(3):
            a, b, c = names(t)
            merge(w, t, 1, a | b)
            back[w, t, 2, a].start()
            merge(w, t, 1, b)
            back[w, t, 2, 0].start()

    def back_two(w):
        for t in range(3):
            a, b, c = names(t)
            merge(w, t, 1, a)
            merge(w, t, 2, a)
            back[w, t, 3, 0].start()

    def back_three(w):
        for t in range(3):
            merge(w, t, 1, 0)
            merge(w, t, 2, 0)
        for t in range(3):
            merge(w, t, 3, 0)
        p = 8 * w
        inv = [1.0 / ac[p, s + 1:s + 2, :] for s in STAT]
        rt = [ac[p, s + 2:s + 3, :] for s in STAT]
        att = jnp.concatenate([ac[p, 0:88, :] * inv[0], ac[p, 96:136, :] * inv[1]], axis=0)
        tan = jnp.concatenate([
            (ac[p, 136:184, :] - att[0:48] * rt[1]) * inv[1],
            (ac[p, 192:272, :] - att[48:128] * rt[2]) * inv[2],
        ], axis=0)
        fin[w, 0] = jnp.transpose(att)
        fin[w, 1] = jnp.transpose(tan)

    outs = [pltpu.make_async_copy(fin.at[0, i], out.at[:, mine], f_o.at[i])
            for i, out in enumerate((o, ot))]
    gifts = [pltpu.make_async_remote_copy(
        src_ref=fin.at[1, i], dst_ref=out.at[:, mine], send_sem=f_s.at[i],
        recv_sem=f_r.at[i], device_id=mate, device_id_type=MESH)
        for i, out in enumerate((o, ot))]

    for c in owns:
        c.wait()
    begin(qmsg[0])
    kbegin(0)
    prep_q(0, 1)
    pass_first(qmsg[0])
    prep_k(0, 1)
    for i in range(2):
        swaps[i].wait_recv()
    begin(qmsg[1])
    pass_second(qmsg[0])
    kpass(0)
    end_near(qmsg[0])
    prep_q(1, 3)
    tile(0, 0, 1)
    pass_both(qmsg[0])
    pass_first(qmsg[1])
    knear(0)
    pass_second(qmsg[1])
    end_far(qmsg[0])
    prep_q(4, 4)
    for i in range(2, 6):
        swaps[i].wait_recv()
    kbegin(1)
    prep_k(1, 2)
    tile(0, 1, 2)
    kfar(0)
    tile(1, 0, 3)
    pass_both(qmsg[1])
    kpass(1)
    prep_k(3, 2)
    sweep(0, 2, 3, 2)
    end_near(qmsg[1])
    end_far(qmsg[1])
    prep_q(8, 8)
    knear(1)
    tile(2, 0, 5)
    kfar(1)
    tile(3, 0, 5)
    prep_k(5, 3)
    tile(3, 5, 3)
    leave(3)
    tile(2, 5, 3)
    leave(2)
    tile(1, 5, 3)
    leave(1)
    back_one(1)
    tile(0, 5, 3)
    leave(0)
    back_two(1)
    back_one(0)
    back_three(1)
    for c in gifts:
        c.start()
    back_two(0)
    back_three(0)
    for c in outs:
        c.start()
    for c in outs + gifts:
        c.wait()
    for c in swaps + smsg:
        c.wait_send()
    for m in kmsg + qmsg + [back]:
        for c in m.values():
            c.wait_send()


def per_device(queries, keys, values, query_tangent, key_tangent, value_tangent):
    hbm = pl.BlockSpec(memory_space=pl.ANY)
    dma = pltpu.SemaphoreType.DMA
    shape = jax.ShapeDtypeStruct(queries.shape, F32)
    return pl.pallas_call(
        kernel,
        out_shape=(shape, shape),
        in_specs=[hbm] * 6,
        out_specs=(hbm, hbm),
        scratch_shapes=[
            pltpu.VMEM((4, 8, 2, LN, DH), F32),
            pltpu.VMEM((2, 16, LN, DH), F32),
            pltpu.VMEM((2048, 768), BF),
            pltpu.VMEM((2048, 768), BF),
            pltpu.VMEM((256, 2048), BF),
            pltpu.VMEM((256, 2048), BF),
            pltpu.VMEM((2048, 768), BF),
            pltpu.VMEM((2048, 768), BF),
            pltpu.VMEM((16, 280, LN), F32),
            pltpu.VMEM((2, 3, 7, 96, LN), F32),
            pltpu.VMEM((2, 2, LN, DH), F32),
            dma((6,)), dma((6,)), dma((6,)),
            dma((16,)), dma((16,)), dma((48,)), dma((48,)),
            dma((8,)), dma((8,)), dma((42,)), dma((42,)),
            dma((2,)), dma((2,)), dma((2,)),
        ],
        compiler_params=pltpu.CompilerParams(
            collective_id=0, has_side_effects=True, vmem_limit_bytes=62 << 20
        ),
        name="attention_tangent",
    )(queries, query_tangent, keys, key_tangent, values, value_tangent)


def solution(mesh):
    spec = P(("pb", "kv"), None)
    return jax.shard_map(
        per_device, mesh=mesh, in_specs=(spec,) * 6, out_specs=(spec, spec), check_vma=False
    )
```

time: 69.3 us -> 66.9 us (0.965)
  the two profiles are of different devices: /device:TPU:1 before, /device:TPU:0 now
where the time goes in v2:
time: 66.9 us; the launch traced here: 66.8 us
  Pallas kernels  63.8 us (95%)
  local copies, waits for them, and re-layouts  2.26 us (3%)
    pallas_call x1, Pallas kernels, per_device(): pl.pallas_call(kernel, out_shape=(shape, shape), in_specs=[hbm] * 6, out_...  63.8 us
    unnamed x4, local copies, waits for them, and re-layouts  2.26 us

profile of v2, /device:TPU:0, one launch (start us, length us, event | category | flops | bytes accessed | tf_op | source)
XLA Modules:
  0.0 66.8 jit_solution(6946862110847799375)
XLA Ops:
  0.6 63.8 %attention_tangent.1 = (f32[128,256]{1,0:T(8,128)}, f32[128,256]{1,0:T(8,128)}) custom-call(f32[128,256]{1,0:T(8,128)} %q.1, f32[128,256]{1,0:T(8,128)} %dq.1, f32[128,256]{1,0:T(8,128)} %k.1, f32[128,256]{1,0:T(8,128)} %dk.1, f32[128,256]{1,0:T(8,128)} %v.1, f32[128,256]{1,0:T(8,128)} %dv.1), custom_call_target="tpu_custom_call" | custom-call | tf_op jit(solution)/shard_map/attention_tangent/pallas_call | solution.py:393
  64.5 0.0 copy-start
  64.5 1.6 %copy.10 = f32[128,256]{1,0:T(8,128)} copy(f32[128,256]{1,0:T(8,128)} %get-tuple-element.4) | data formatting | bytes 262144
  66.1 0.0 copy-done
  66.1 0.7 copy.11
Async XLA Ops:
  64.5 1.6 %copy-start = (f32[128,256]{1,0:T(8,128)S(1)}, f32[128,256]{1,0:T(8,128)}, u32[]{:S(2)}) copy-start(f32[128,256]{1,0:T(8,128)} %get-tuple-element.5) | copy-start | bytes 393220

commit v3 on v2

--- a/solution.py
+++ b/solution.py
@@ -280,15 +280,17 @@
         ac[p, r0:r0 + n, :] = ac[p, r0:r0 + n, :] * f1 + rb[w, t, i, :n, :] * f2
         ac[p, st:st + 1, :] = top
 
-    def back_one(w):
+    def back_far(w):
         for t in range(3):
             a, b, c = names(t)
             merge(w, t, 1, a | b)
             back[w, t, 2, a].start()
+
+    def back_near(w):
+        for t in range(3):
+            a, b, c = names(t)
             merge(w, t, 1, b)
             back[w, t, 2, 0].start()
-
-    def back_two(w):
         for t in range(3):
             a, b, c = names(t)
             merge(w, t, 1, a)
@@ -346,8 +348,8 @@
     prep_k(1, 2)
     tile(0, 1, 2)
     kfar(0)
+    pass_both(qmsg[1])
     tile(1, 0, 3)
-    pass_both(qmsg[1])
     kpass(1)
     prep_k(3, 2)
     sweep(0, 2, 3, 2)
@@ -363,17 +365,17 @@
     leave(3)
     tile(2, 5, 3)
     leave(2)
+    back_far(1)
     tile(1, 5, 3)
     leave(1)
-    back_one(1)
+    back_near(1)
     tile(0, 5, 3)
     leave(0)
-    back_two(1)
-    back_one(0)
+    back_far(0)
+    back_near(0)
     back_three(1)
     for c in gifts:
         c.start()
-    back_two(0)
     back_three(0)
     for c in outs:
         c.start()

time: 66.9 us -> 66 us (0.987)
  Pallas kernels: 63.8 us -> 63 us
    pallas_call x1, Pallas kernels: 63.8 us -> 63 us  [per_device(): pl.pallas_call(kernel, out_shape=(shape, shape), in_specs=[hbm] * 6, out_...]
where the time goes in v3:
time: 66 us; the launch traced here: 65.9 us
  Pallas kernels  63 us (95%)
  local copies, waits for them, and re-layouts  2.26 us (3%)
    pallas_call x1, Pallas kernels, per_device(): pl.pallas_call(kernel, out_shape=(shape, shape), in_specs=[hbm] * 6, out_...  63 us
    unnamed x4, local copies, waits for them, and re-layouts  2.26 us

profile of v3, /device:TPU:0, one launch (start us, length us, event | category | flops | bytes accessed | tf_op | source)
XLA Modules:
  0.0 65.9 jit_solution(222499063999470234)
XLA Ops:
  0.6 63.0 %attention_tangent.1 = (f32[128,256]{1,0:T(8,128)}, f32[128,256]{1,0:T(8,128)}) custom-call(f32[128,256]{1,0:T(8,128)} %q.1, f32[128,256]{1,0:T(8,128)} %dq.1, f32[128,256]{1,0:T(8,128)} %k.1, f32[128,256]{1,0:T(8,128)} %dk.1, f32[128,256]{1,0:T(8,128)} %v.1, f32[128,256]{1,0:T(8,128)} %dv.1), custom_call_target="tpu_custom_call" | custom-call | tf_op jit(solution)/shard_map/attention_tangent/pallas_call | solution.py:395
  63.6 0.0 copy-start
  63.6 1.6 %copy.10 = f32[128,256]{1,0:T(8,128)} copy(f32[128,256]{1,0:T(8,128)} %get-tuple-element.4) | data formatting | bytes 262144
  65.2 0.0 copy-done
  65.2 0.7 copy.11
Async XLA Ops:
  63.6 1.6 %copy-start = (f32[128,256]{1,0:T(8,128)S(1)}, f32[128,256]{1,0:T(8,128)}, u32[]{:S(2)}) copy-start(f32[128,256]{1,0:T(8,128)} %get-tuple-element.5) | copy-start | bytes 393220

commit v4 on v3

--- a/solution.py
+++ b/solution.py
@@ -38,8 +38,9 @@
     return hi, mid, (rest - mid.astype(F32)).astype(BF)
 
 
-def kernel(q, dq, k, dk, v, dv, o, ot, kvb, qb, ks, ky, vh, vl, qs, qx, ac, rb, fin,
+def kernel(q, dq, k, dk, v, dv, oo, kvb, qb, ks, ky, vh, vl, qs, qx, ac, rb, fin,
            swap_s, swap_r, own_s, k_s, k_r, q_s, q_r, s_s, s_r, b_s, b_r, f_s, f_r, f_o):
+    o, ot = oo.at[0], oo.at[1]
     pb, kv = lax.axis_index("pb"), lax.axis_index("kv")
     core, x = pb % 2, pb // 4
     z, y = (kv // 4) * 2 + (pb // 2) % 2, kv % 4
@@ -328,50 +329,51 @@
     prep_q(0, 1)
     pass_first(qmsg[0])
     prep_k(0, 1)
-    for i in range(2):
-        swaps[i].wait_recv()
-    begin(qmsg[1])
     pass_second(qmsg[0])
     kpass(0)
     end_near(qmsg[0])
     prep_q(1, 3)
+    pass_both(qmsg[0])
+    for i in range(2):
+        swaps[i].wait_recv()
+    begin(qmsg[1])
     tile(0, 0, 1)
-    pass_both(qmsg[0])
-    pass_first(qmsg[1])
     knear(0)
-    pass_second(qmsg[1])
-    end_far(qmsg[0])
-    prep_q(4, 4)
     for i in range(2, 6):
         swaps[i].wait_recv()
     kbegin(1)
     prep_k(1, 2)
     tile(0, 1, 2)
+    pass_first(qmsg[1])
+    end_far(qmsg[0])
+    prep_q(4, 4)
     kfar(0)
+    tile(1, 0, 3)
+    pass_second(qmsg[1])
+    kpass(1)
     pass_both(qmsg[1])
-    tile(1, 0, 3)
-    kpass(1)
     prep_k(3, 2)
     sweep(0, 2, 3, 2)
     end_near(qmsg[1])
+    prep_q(8, 4)
+    tile(2, 0, 5)
+    knear(1)
     end_far(qmsg[1])
-    prep_q(8, 8)
-    knear(1)
-    tile(2, 0, 5)
+    prep_q(12, 4)
+    tile(3, 0, 5)
     kfar(1)
-    tile(3, 0, 5)
     prep_k(5, 3)
     tile(3, 5, 3)
     leave(3)
+    tile(1, 5, 3)
+    leave(1)
+    back_far(1)
     tile(2, 5, 3)
     leave(2)
-    back_far(1)
-    tile(1, 5, 3)
-    leave(1)
+    back_far(0)
     back_near(1)
     tile(0, 5, 3)
     leave(0)
-    back_far(0)
     back_near(0)
     back_three(1)
     for c in gifts:
@@ -391,12 +393,12 @@
 def per_device(queries, keys, values, query_tangent, key_tangent, value_tangent):
     hbm = pl.BlockSpec(memory_space=pl.ANY)
     dma = pltpu.SemaphoreType.DMA
-    shape = jax.ShapeDtypeStruct(queries.shape, F32)
-    return pl.pallas_call(
+    shape = jax.ShapeDtypeStruct((2,) + queries.shape, F32)
+    both = pl.pallas_call(
         kernel,
-        out_shape=(shape, shape),
+        out_shape=shape,
         in_specs=[hbm] * 6,
-        out_specs=(hbm, hbm),
+        out_specs=hbm,
         scratch_shapes=[
             pltpu.VMEM((4, 8, 2, LN, DH), F32),
             pltpu.VMEM((2, 16, LN, DH), F32),
@@ -419,6 +421,7 @@
         ),
         name="attention_tangent",
     )(queries, query_tangent, keys, key_tangent, values, value_tangent)
+    return both[0], both[1]
 
 
 def solution(mesh):

time: 66 us -> 65.6 us (level)
    unnamed x4 -> x0, local copies, waits for them, and re-layouts: 2.26 us -> none
    squeeze x0 -> x1, local copies, waits for them, and re-layouts: none -> 1.69 us  [per_device(): return (both[0], both[1])]
where the time goes in v4:
time: 65.6 us; the launch traced here: 65 us
  Pallas kernels  62.7 us (96%)
  local copies, waits for them, and re-layouts  1.69 us (3%)
    pallas_call x1, Pallas kernels, per_device(): pl.pallas_call(kernel, out_shape=shape, in_specs=[hbm] * 6, out_specs=hbm...  62.7 us
    squeeze x1, local copies, waits for them, and re-layouts, per_device(): return (both[0], both[1])  1.69 us

profile of v4, /device:TPU:0, one launch (start us, length us, event | category | flops | bytes accessed | tf_op | source)
XLA Modules:
  0.0 65.0 jit_solution(1426064263208146811)
XLA Ops:
  0.6 62.7 %attention_tangent.1 = f32[2,128,256]{2,1,0:T(8,128)} custom-call(f32[128,256]{1,0:T(8,128)} %q.1, f32[128,256]{1,0:T(8,128)} %dq.1, f32[128,256]{1,0:T(8,128)} %k.1, f32[128,256]{1,0:T(8,128)} %dk.1, f32[128,256]{1,0:T(8,128)} %v.1, f32[128,256]{1,0:T(8,128)} %dv.1), custom_call_target="tpu_custom_call" | custom-call | tf_op jit(solution)/shard_map/attention_tangent/pallas_call | solution.py:397
  63.3 1.7 %slice_bitcast_fusion = (f32[128,256]{1,0:T(8,128)}, f32[128,256]{1,0:T(8,128)}) fusion(f32[2,128,256]{2,1,0:T(8,128)} %attention_tangent.1), kind=kLoop, calls=%fused_computation | loop fusion | bytes 524288 | tf_op jit(solution)/shard_map/squeeze | solution.py:424

commit v5 on v4

--- a/solution.py
+++ b/solution.py
@@ -354,19 +354,19 @@
     pass_both(qmsg[1])
     prep_k(3, 2)
     sweep(0, 2, 3, 2)
+    knear(1)
     end_near(qmsg[1])
-    prep_q(8, 4)
-    tile(2, 0, 5)
-    knear(1)
     end_far(qmsg[1])
-    prep_q(12, 4)
-    tile(3, 0, 5)
+    prep_q(8, 8)
+    tile(3, 0, 3)
     kfar(1)
+    tile(3, 3, 2)
     prep_k(5, 3)
     tile(3, 5, 3)
     leave(3)
     tile(1, 5, 3)
     leave(1)
+    tile(2, 0, 5)
     back_far(1)
     tile(2, 5, 3)
     leave(2)

time: 65.6 us -> 61.1 us (0.931)
  Pallas kernels: 62.7 us -> 58.7 us
    pallas_call x1, Pallas kernels: 62.7 us -> 58.7 us  [per_device(): pl.pallas_call(kernel, out_shape=shape, in_specs=[hbm] * 6, out_specs=hbm...]
where the time goes in v5:
time: 61.1 us; the launch traced here: 61 us
  Pallas kernels  58.7 us (96%)
  local copies, waits for them, and re-layouts  1.69 us (3%)
  between operations  0.64 us (1%)
    pallas_call x1, Pallas kernels, per_device(): pl.pallas_call(kernel, out_shape=shape, in_specs=[hbm] * 6, out_specs=hbm...  58.7 us
    squeeze x1, local copies, waits for them, and re-layouts, per_device(): return (both[0], both[1])  1.69 us

profile of v5, /device:TPU:0, one launch (start us, length us, event | category | flops | bytes accessed | tf_op | source)
XLA Modules:
  0.0 61.0 jit_solution(7150624422428995164)
XLA Ops:
  0.6 58.7 %attention_tangent.1 = f32[2,128,256]{2,1,0:T(8,128)} custom-call(f32[128,256]{1,0:T(8,128)} %q.1, f32[128,256]{1,0:T(8,128)} %dq.1, f32[128,256]{1,0:T(8,128)} %k.1, f32[128,256]{1,0:T(8,128)} %dk.1, f32[128,256]{1,0:T(8,128)} %v.1, f32[128,256]{1,0:T(8,128)} %dv.1), custom_call_target="tpu_custom_call" | custom-call | tf_op jit(solution)/shard_map/attention_tangent/pallas_call | solution.py:397
  59.3 1.7 %slice_bitcast_fusion = (f32[128,256]{1,0:T(8,128)}, f32[128,256]{1,0:T(8,128)}) fusion(f32[2,128,256]{2,1,0:T(8,128)} %attention_tangent.1), kind=kLoop, calls=%fused_computation | loop fusion | bytes 524288 | tf_op jit(solution)/shard_map/squeeze | solution.py:424

commit v6 on v5

--- a/solution.py
+++ b/solution.py
@@ -29,13 +29,6 @@
 def two(x):
     hi = x.astype(BF)
     return hi, (x - hi.astype(F32)).astype(BF)
-
-
-def three(x):
-    hi = x.astype(BF)
-    rest = x - hi.astype(F32)
-    mid = rest.astype(BF)
-    return hi, mid, (rest - mid.astype(F32)).astype(BF)
 
 
 def kernel(q, dq, k, dk, v, dv, oo, kvb, qb, ks, ky, vh, vl, qs, qx, ac, rb, fin,
@@ -176,9 +169,9 @@
 
         def one(i, _):
             r = pl.ds(pl.multiple_of(i * 256, 256), 256)
-            kh, km, kl = three(kvb[0, i].reshape(256, DH))
+            kh, km = two(kvb[0, i].reshape(256, DH))
             dh, dm = two(kvb[1, i].reshape(256, DH))
-            ks[r, :] = jnp.concatenate([kh, km, kh, km, kl, kh], axis=1)
+            ks[r, :] = jnp.concatenate([kh, km, kh, km], axis=1)
             ky[r, :] = jnp.concatenate([kh, dh, km, dm, kh, dh], axis=1)
             for a in range(2):
                 hi, lo = two(jnp.transpose(kvb[2 + a, i].reshape(256, DH)))
@@ -191,8 +184,8 @@
         def one(i, _):
             r = pl.ds(pl.multiple_of(i * LN, LN), LN)
             raw = qb[0, i]
-            h, m, l = three(raw * base2)
-            qs[r, :] = jnp.concatenate([h, h, m, m, h, l], axis=1)
+            h, m = two(raw * base2)
+            qs[r, :] = jnp.concatenate([h, h, m, m], axis=1)
             h, m = two(raw * root)
             dh, dm = two(qb[1, i] * root)
             qx[r, :] = jnp.concatenate([dh, h, dh, h, dm, m], axis=1)
@@ -402,11 +395,11 @@
         scratch_shapes=[
             pltpu.VMEM((4, 8, 2, LN, DH), F32),
             pltpu.VMEM((2, 16, LN, DH), F32),
-            pltpu.VMEM((2048, 768), BF),
+            pltpu.VMEM((2048, 512), BF),
             pltpu.VMEM((2048, 768), BF),
             pltpu.VMEM((256, 2048), BF),
             pltpu.VMEM((256, 2048), BF),
-            pltpu.VMEM((2048, 768), BF),
+            pltpu.VMEM((2048, 512), BF),
             pltpu.VMEM((2048, 768), BF),
             pltpu.VMEM((16, 280, LN), F32),
             pltpu.VMEM((2, 3, 7, 96, LN), F32),

time: 61.1 us -> 59.2 us (0.969)
  Pallas kernels: 58.7 us -> 56.7 us
    pallas_call x1, Pallas kernels: 58.7 us -> 56.7 us  [per_device(): pl.pallas_call(kernel, out_shape=shape, in_specs=[hbm] * 6, out_specs=hbm...]
where the time goes in v6:
time: 59.2 us; the launch traced here: 59 us
  Pallas kernels  56.7 us (96%)
  local copies, waits for them, and re-layouts  1.69 us (3%)
  between operations  0.64 us (1%)
    pallas_call x1, Pallas kernels, per_device(): pl.pallas_call(kernel, out_shape=shape, in_specs=[hbm] * 6, out_specs=hbm...  56.7 us
    squeeze x1, local copies, waits for them, and re-layouts, per_device(): return (both[0], both[1])  1.69 us

profile of v6, /device:TPU:0, one launch (start us, length us, event | category | flops | bytes accessed | tf_op | source)
XLA Modules:
  0.0 59.0 jit_solution(18343234226887372613)
XLA Ops:
  0.6 56.7 %attention_tangent.1 = f32[2,128,256]{2,1,0:T(8,128)} custom-call(f32[128,256]{1,0:T(8,128)} %q.1, f32[128,256]{1,0:T(8,128)} %dq.1, f32[128,256]{1,0:T(8,128)} %k.1, f32[128,256]{1,0:T(8,128)} %dk.1, f32[128,256]{1,0:T(8,128)} %v.1, f32[128,256]{1,0:T(8,128)} %dv.1), custom_call_target="tpu_custom_call" | custom-call | tf_op jit(solution)/shard_map/attention_tangent/pallas_call | solution.py:390
  57.3 1.7 %slice_bitcast_fusion = (f32[128,256]{1,0:T(8,128)}, f32[128,256]{1,0:T(8,128)}) fusion(f32[2,128,256]{2,1,0:T(8,128)} %attention_tangent.1), kind=kLoop, calls=%fused_computation | loop fusion | bytes 524288 | tf_op jit(solution)/shard_map/squeeze | solution.py:417

commit v7 on v6

--- a/solution.py
+++ b/solution.py
@@ -133,39 +133,46 @@
             send_sem=k_s.at[i], recv_sem=k_r.at[i], device_id=kn[d], device_id_type=MESH)
 
     kmsg = [{(t, to): kroute(w, t, to) for t in range(2) for to in range(1, 4)} for w in range(2)]
-    smsg = [pltpu.make_async_remote_copy(
-        src_ref=kvb.at[:, i, 0], dst_ref=kvb.at[:, i, 1], send_sem=s_s.at[i],
-        recv_sem=s_r.at[i], device_id=sib, device_id_type=MESH) for i in range(8)]
+    def handed(i, t):
+        part = pl.ds(64 * t, 64)
+        return pltpu.make_async_remote_copy(
+            src_ref=kvb.at[:, i, 0, part], dst_ref=kvb.at[:, i, 1, part],
+            send_sem=s_s.at[2 * i + t], recv_sem=s_r.at[2 * i + t],
+            device_id=sib, device_id_type=MESH)
+
+    smsg = [[handed(i, t) for t in range(2)] for i in range(8)]
 
     def kbegin(w):
         for t in range(2):
             kmsg[w][t, 1 << t].start()
         for t in range(2):
             kmsg[w][t, 2 >> t].start()
-        smsg[4 * w].start()
+        for c in smsg[4 * w]:
+            c.start()
 
     def kpass(w):
         for t in range(2):
             kmsg[w][t, 1 << t].wait_recv()
             kmsg[w][t, 3].start()
+            smsg[4 * w + (1 << t)][t].start()
 
     def knear(w):
         for t in range(2):
             kmsg[w][t, 2 >> t].wait_recv()
-        smsg[4 * w + 1].start()
-        smsg[4 * w + 2].start()
+            smsg[4 * w + (2 >> t)][t].start()
 
     def kfar(w):
         for t in range(2):
             kmsg[w][t, 3].wait_recv()
-        smsg[4 * w + 3].start()
+            smsg[4 * w + 3][t].start()
 
     root = 1.0 / math.sqrt(DH)
     base2 = root * math.log2(math.e)
 
     def prep_k(first, count):
         for i in range(first, first + count):
-            smsg[i].wait_recv()
+            for c in smsg[i]:
+                c.wait_recv()
 
         def one(i, _):
             r = pl.ds(pl.multiple_of(i * 256, 256), 256)
@@ -376,7 +383,7 @@
         c.start()
     for c in outs + gifts:
         c.wait()
-    for c in swaps + smsg:
+    for c in swaps + sum(smsg, []):
         c.wait_send()
     for m in kmsg + qmsg + [back]:
         for c in m.values():
@@ -406,7 +413,7 @@
             pltpu.VMEM((2, 2, LN, DH), F32),
             dma((6,)), dma((6,)), dma((6,)),
             dma((16,)), dma((16,)), dma((48,)), dma((48,)),
-            dma((8,)), dma((8,)), dma((42,)), dma((42,)),
+            dma((16,)), dma((16,)), dma((42,)), dma((42,)),
             dma((2,)), dma((2,)), dma((2,)),
         ],
         compiler_params=pltpu.CompilerParams(

time: 59.2 us -> 59.3 us (level)
  no operation moved by 1% of the time
where the time goes in v7:
time: 59.3 us; the launch traced here: 59 us
  Pallas kernels  56.6 us (95%)
  local copies, waits for them, and re-layouts  1.69 us (3%)
  between operations  0.64 us (1%)
    pallas_call x1, Pallas kernels, per_device(): pl.pallas_call(kernel, out_shape=shape, in_specs=[hbm] * 6, out_specs=hbm...  56.6 us
    squeeze x1, local copies, waits for them, and re-layouts, per_device(): return (both[0], both[1])  1.69 us

profile of v7, /device:TPU:0, one launch (start us, length us, event | category | flops | bytes accessed | tf_op | source)
XLA Modules:
  0.0 59.0 jit_solution(3023064597139117797)
XLA Ops:
  0.6 56.6 %attention_tangent.1 = f32[2,128,256]{2,1,0:T(8,128)} custom-call(f32[128,256]{1,0:T(8,128)} %q.1, f32[128,256]{1,0:T(8,128)} %dq.1, f32[128,256]{1,0:T(8,128)} %k.1, f32[128,256]{1,0:T(8,128)} %dk.1, f32[128,256]{1,0:T(8,128)} %v.1, f32[128,256]{1,0:T(8,128)} %dv.1), custom_call_target="tpu_custom_call" | custom-call | tf_op jit(solution)/shard_map/attention_tangent/pallas_call | solution.py:397
  57.3 1.7 %slice_bitcast_fusion = (f32[128,256]{1,0:T(8,128)}, f32[128,256]{1,0:T(8,128)}) fusion(f32[2,128,256]{2,1,0:T(8,128)} %attention_tangent.1), kind=kLoop, calls=%fused_computation | loop fusion | bytes 524288 | tf_op jit(solution)/shard_map/squeeze | solution.py:424
